TPU v7x, 32 devices: a whole 2x2x4 slice. The times are simulated.
32 devices in a mesh: pool: 1, fsdp: 32 (over z, y, x, core).
Axes of the slice: x: 2, y: 2, z: 4, core: 2. Of those that a mesh axis runs over, the one named last changes fastest.
Arguments:
- noisy: bfloat16 [2048, 2560], P(('pool', 'fsdp')), may hold values from -6 to 6
- clean: bfloat16 [2048, 2560], P(('pool', 'fsdp')), may hold values from -6 to 6
- seg_ids: int32 [32], P('pool'), may hold values from 0 to 3, never falling along the last dimension, each value on 1 to 12 neighbouring positions
- lag_mask: int32 [32, 2], P(('pool', 'fsdp')), may hold values 0 or 1
- plan: int32 [32, 2], P(('pool', 'fsdp')), may hold values from 1 to 999, as said below
- w_query: bfloat16 [2560, 2560], P('fsdp'), may hold values from -0.125 to 0.125
- w_key: bfloat16 [2560, 2560], P('fsdp'), may hold values from -0.125 to 0.125
- time_proj: bfloat16 [128, 7680], replicated, may hold values from -0.5 to 0.5
- q_gain: float32 [2560], replicated, may hold values from 0.5 to 14
- k_gain: float32 [2560], replicated, may hold values from 0.5 to 14
Outputs:
- denoised: bfloat16 [2048, 2560], P(('pool', 'fsdp'))
Inputs may be any that keep to these rules, and one draw needn't show every extreme that they name: seg_ids never falls along the spans; each rollout is 1 to 12 consecutive spans. `plan`: entry j of a row lies from 1000 * (1 - j) // 2 + 1 to 1000 * (2 - j) // 2 - 1, so each row falls strictly.
All inputs are finite; a program needn't handle non-finite values. No bound on the sum of `lag_mask` on one device may be relied on, other than what follows from the above.
Results may differ from a plain program's by a relative error of at most 0.024.
Values may be sent and summed in bfloat16 or wider, within the bound.
No kernel may reach another device: no remote copies, remote signals or barrier semaphores. Data moves between devices by JAX's collectives and lax.ppermute only.
A program may use at most 128 MiB of HBM per device.

v0:
```python
import math
import jax
import jax.numpy as jnp
from jax import lax
from jax.sharding import PartitionSpec as P

HEADS = 20
HEAD_DIM = 128
STEPS = 2
LAGS = 2
LEVELS = 1000
SIGMA_SHIFT = 5.0
EPSILON = 1e-06
MASKED = -1e30


def passed_along(value, axis, steps):
    count = lax.axis_size(axis)
    leading, last = (max(0, -steps), min(count, count - steps))
    return lax.ppermute(value, axis, [(source, source + steps) for source in range(leading, last)])


def sigma_of(levels):
    fraction = levels.astype(jnp.float32) / LEVELS
    return SIGMA_SHIFT * fraction / (1.0 + (SIGMA_SHIFT - 1.0) * fraction)


def frequencies(half_count):
    return jnp.exp(-math.log(10000.0) * jnp.arange(half_count, dtype=jnp.float32) / half_count)


def modulation(sigmas, time_proj):
    half_count = time_proj.shape[0] // 2
    angles = 1000.0 * sigmas[:, None] * frequencies(half_count)[None, :]
    features = jnp.concatenate([jnp.cos(angles), jnp.sin(angles)], axis=1).astype(jnp.bfloat16)
    return jnp.dot(features, time_proj, preferred_element_type=jnp.float32)[0]


def modulate(latent, mod_row, model_width):
    values = latent.astype(jnp.float32)
    centred = values - jnp.mean(values, axis=-1, keepdims=True)
    variance = jnp.mean(centred * centred, axis=-1, keepdims=True)
    normed = centred * lax.rsqrt(variance + EPSILON)
    return (normed * (1.0 + mod_row[model_width : 2 * model_width]) + mod_row[:model_width]).astype(
        jnp.bfloat16
    )


def normalize(values, gain):
    mean_square = jnp.mean(values * values, axis=-1, keepdims=True)
    return values * lax.rsqrt(mean_square + EPSILON) * gain


def rotate(values, positions):
    half_count = HEAD_DIM // 2
    split_heads = values.reshape(values.shape[:-1] + (HEADS, HEAD_DIM))
    angles = positions[..., None] * frequencies(half_count)
    cosine = jnp.cos(angles)[..., None, :]
    sine = jnp.sin(angles)[..., None, :]
    front = split_heads[..., :half_count]
    back = split_heads[..., half_count:]
    turned = jnp.concatenate([front * cosine - back * sine, front * sine + back * cosine], axis=-1)
    return turned.reshape(values.shape)


def attend(query_rows, key_rows, value_rows, usable):
    row_count = query_rows.shape[0]
    query_heads = query_rows.reshape(row_count, HEADS, HEAD_DIM)
    key_heads = key_rows.reshape(-1, HEADS, HEAD_DIM)
    value_heads = value_rows.reshape(-1, HEADS, HEAD_DIM)
    scores = jnp.einsum(
        "qhd,khd->hqk", query_heads, key_heads, preferred_element_type=jnp.float32
    ) * HEAD_DIM ** (-0.5)
    scores = jnp.where(usable[None, None, :], scores, MASKED)
    highest = jnp.max(scores, axis=-1, keepdims=True)
    expanded = jnp.exp(scores - highest)
    weights = (expanded / jnp.sum(expanded, axis=-1, keepdims=True)).astype(jnp.bfloat16)
    mixed = jnp.einsum("hqk,khd->qhd", weights, value_heads, preferred_element_type=jnp.float32)
    return mixed.reshape(row_count, HEADS * HEAD_DIM).astype(jnp.bfloat16)


def make_absorbers(noisy_hidden, context_hidden):

    def absorb_both(carry, pieces, offset):
        stored = tuple((piece_rows for piece_rows in pieces))
        query_sum = jnp.dot(noisy_hidden, pieces[0], preferred_element_type=jnp.float32)
        key_sum = jnp.dot(noisy_hidden, pieces[1], preferred_element_type=jnp.float32)
        ctxkey_sum = jnp.dot(context_hidden, pieces[1], preferred_element_type=jnp.float32)
        return (stored, (query_sum, key_sum, ctxkey_sum))

    def absorb_key(carry, piece, offset):
        buffer_rows, partials = carry
        stored = lax.dynamic_update_slice_in_dim(buffer_rows, piece, offset, 0)
        key_sum, ctxkey_sum = partials
        key_sum = key_sum + jnp.dot(noisy_hidden, piece, preferred_element_type=jnp.float32)
        ctxkey_sum = ctxkey_sum + jnp.dot(context_hidden, piece, preferred_element_type=jnp.float32)
        return (stored, (key_sum, ctxkey_sum))

    def absorb_query(carry, piece, offset):
        buffer_rows, query_sum = carry
        stored = lax.dynamic_update_slice_in_dim(buffer_rows, piece, offset, 0)
        query_sum = query_sum + jnp.dot(noisy_hidden, piece, preferred_element_type=jnp.float32)
        return (stored, query_sum)

    return (absorb_both, absorb_key, absorb_query)


def local(noisy, clean, seg_ids, lag_mask, plan, w_query, w_key, time_proj, q_gain, k_gain):
    row_count, model_width = noisy.shape
    inner_width = w_query.shape[1]
    span_index = lax.axis_index("fsdp")
    segment_start = jnp.sum((seg_ids < seg_ids[span_index]).astype(jnp.int32))
    span_place = span_index - segment_start
    positions = (span_place * row_count + jnp.arange(row_count, dtype=jnp.int32)).astype(
        jnp.float32
    )
    sigmas = [sigma_of(plan[0, level_index : level_index + 1]) for level_index in range(STEPS)] + [
        jnp.zeros((1,), jnp.float32)
    ]
    rest_mod = modulation(jnp.zeros((1,), jnp.float32), time_proj)
    step_mods = [modulation(sigmas[level_index], time_proj) for level_index in range(STEPS)]
    context_hidden = modulate(clean, rest_mod, model_width)
    noisy_hidden = modulate(noisy, step_mods[0], model_width)
    absorb_both, absorb_key, absorb_query = make_absorbers(noisy_hidden, context_hidden)
    empty_buffer = jnp.zeros((model_width, inner_width), jnp.bfloat16)
    empty_sum = jnp.zeros((row_count, inner_width), jnp.float32)
    buffers, partials = absorb_both(
        ((empty_buffer, empty_buffer), (empty_sum, empty_sum, empty_sum)),
        (
            lax.all_gather(w_query, "fsdp", axis=0, tiled=True),
            lax.all_gather(w_key, "fsdp", axis=0, tiled=True),
        ),
        jnp.int32(0),
    )
    full_query, full_key = buffers
    query_sum, key_sum, ctxkey_sum = partials
    context_key = rotate(normalize(ctxkey_sum, k_gain), positions).astype(jnp.bfloat16)
    context_pair = jnp.stack([context_key, context_hidden])
    received = [passed_along(context_pair, "fsdp", 1)]
    distance = 2
    received.append(passed_along(context_pair, "fsdp", distance))
    usable_parts = [jnp.ones((row_count,), jnp.int32) > 0]
    for distance in range(1, LAGS + 1):
        source = jnp.maximum(span_index - distance, 0)
        allowed = (
            (span_index >= distance)
            & (seg_ids[source] == seg_ids[span_index])
            & (lag_mask[0, distance - 1] == 1)
        )
        usable_parts.append(jnp.broadcast_to(allowed, (row_count,)))
    usable = jnp.concatenate(usable_parts)
    keys_context = jnp.concatenate([pair_rows[0] for pair_rows in received], axis=0)
    values_context = jnp.concatenate([pair_rows[1] for pair_rows in received], axis=0)
    latent = noisy
    for step_index in range(STEPS):
        if step_index == 0:
            hidden = noisy_hidden
            query_raw, key_raw = (query_sum, key_sum)
        else:
            hidden = modulate(latent, step_mods[step_index], model_width)
            query_raw = jnp.dot(hidden, full_query, preferred_element_type=jnp.float32)
            key_raw = jnp.dot(hidden, full_key, preferred_element_type=jnp.float32)
        query_rows = rotate(normalize(query_raw, q_gain), positions).astype(jnp.bfloat16)
        key_rows = rotate(normalize(key_raw, k_gain), positions).astype(jnp.bfloat16)
        mixed = attend(
            query_rows,
            jnp.concatenate([key_rows, keys_context], axis=0),
            jnp.concatenate([hidden, values_context], axis=0),
            usable,
        )
        sigma_change = sigmas[step_index + 1] - sigmas[step_index]
        factor = sigma_change * step_mods[step_index][2 * model_width :]
        latent = (latent.astype(jnp.float32) + factor[None, :] * mixed.astype(jnp.float32)).astype(
            jnp.bfloat16
        )
    return latent


def solution(mesh):
    placed = (
        P(("pool", "fsdp"), None),
        P(("pool", "fsdp"), None),
        P("pool"),
        P(("pool", "fsdp"), None),
        P(("pool", "fsdp"), None),
        P("fsdp", None),
        P("fsdp", None),
        P(),
        P(),
        P(),
    )
    return jax.shard_map(
        local, mesh=mesh, in_specs=placed, out_specs=P(("pool", "fsdp"), None), check_vma=False
    )
```

profile of v0, /device:TPU:9, one launch (start us, length us, event | category | flops | bytes accessed | tf_op | source)
XLA Modules:
  0.0 298.8 jit_solution(1294598367972171601)
XLA Ops:
  8.0 1.3 fusion.99
  10.8 1.4 fusion.101
  12.2 2.0 fusion.50
  17.5 1.4 fusion.100
  21.0 1.1 convert_reduce_fusion.1
  23.3 1.2 fusion.30
  26.9 82.3 %all-gather.3.cloned.1.call-done = bf16[2560,2560]{1,0:T(8,128)(2,1)} async-done(((bf16[80,2560]{1,0:T(8,128)(2,1)}), bf16[2560,2560]{1,0:T(8,128)(2,1)}) %all-gather.3.cloned.1.call-update) | async-done | bytes 13107216 | tf_op jit(solution)/shard_map/all_gather | solution.py:131
  109.2 7.4 %multiply_reduce_fusion.2 = (f32[64]{0:T(128)S(1)}, f32[64,2560]{1,0:T(8,128)S(1)}) fusion(bf16[2560,2560]{1,0:T(8,128)(2,1)} %all-gather.3.cloned.1.call-done, bf16[64,2560]{1,0:T(8,128)(2,1)S(1)} %copy-done.2, f32[2560]{0:T(1024)S(1)} %get-tuple-element.41, f32[2560]{0:T(1024)S(1)} %get-tuple-element.42, f32[64]{0:T(128)S(1)} %add_rsqrt_fusion.7, ...), kind=kOutput, calls=%fused_computation.79 | convolution fusion | flops 840171456 | bytes 14111488 | tf_op jit(solution)/shard_map/dot_general | solution.py:87
  117.6 2.5 multiply_reduce_fusion.4
  122.2 1.2 reshape.303
  123.3 2.8 fusion.95
  126.2 1.4 fusion.96
  127.5 80.8 %all-gather.5.cloned.1.call-done = bf16[2560,2560]{1,0:T(8,128)(2,1)} async-done(((bf16[80,2560]{1,0:T(8,128)(2,1)}), bf16[2560,2560]{1,0:T(8,128)(2,1)}) %all-gather.5.cloned.1.call-update) | async-done | bytes 13107216 | tf_op jit(solution)/shard_map/all_gather | solution.py:130
  208.3 7.3 %multiply_reduce_fusion.3 = (f32[64]{0:T(128)S(1)}, f32[64,2560]{1,0:T(8,128)S(1)}) fusion(bf16[2560,2560]{1,0:T(8,128)(2,1)} %all-gather.5.cloned.1.call-done, bf16[64,2560]{1,0:T(8,128)(2,1)S(1)} %copy-done.2, f32[2560]{0:T(1024)S(1)} %get-tuple-element.41, f32[2560]{0:T(1024)S(1)} %get-tuple-element.42, f32[64]{0:T(128)S(1)} %add_rsqrt_fusion.7, ...), kind=kOutput, calls=%fused_computation.83 | convolution fusion | flops 840171456 | bytes 14111488 | tf_op jit(solution)/shard_map/dot_general | solution.py:86
  216.6 1.2 reshape.304
  219.6 1.8 subtract_convert_fusion.3
  223.3 3.2 %collective-permute-start = (bf16[2,64,2560]{2,1,0:T(8,128)(2,1)}, bf16[2,64,2560]{2,1,0:T(8,128)(2,1)S(1)}, u32[]{:S(2)}, u32[]{:S(2)}) collective-permute-start(bf16[2,64,2560]{2,1,0:T(8,128)(2,1)} %pad_maximum_fusion.12), channel_id=1, source_target_pairs={{0,1},{1,2},{2,3},{3,4},{4,5},{5,6},{6,7},{7,8},{8,9},{9,10},{10,1... | collective-permute-start | bytes 1966088 | tf_op jit(solution)/shard_map/ppermute | solution.py:20
  228.0 3.3 %collective-permute-start.1 = (bf16[2,64,2560]{2,1,0:T(8,128)(2,1)}, bf16[2,64,2560]{2,1,0:T(8,128)(2,1)}, u32[]{:S(2)}, u32[]{:S(2)}) collective-permute-start(bf16[2,64,2560]{2,1,0:T(8,128)(2,1)} %pad_maximum_fusion.12), channel_id=1, source_target_pairs={{0,2},{1,3},{2,4},{3,5},{4,6},{5,7},{6,8},{7,9},{8,10},{9,11},{10,... | collective-permute-start | bytes 1966088 | tf_op jit(solution)/shard_map/ppermute | solution.py:20
  231.3 5.8 %collective-permute-done = bf16[2,64,2560]{2,1,0:T(8,128)(2,1)S(1)} collective-permute-done((bf16[2,64,2560]{2,1,0:T(8,128)(2,1)}, bf16[2,64,2560]{2,1,0:T(8,128)(2,1)S(1)}, u32[]{:S(2)}, u32[]{:S(2)}) %collective-permute-start) | collective-permute-done | bytes 655392 | tf_op jit(solution)/shard_map/ppermute | solution.py:20
  238.2 12.7 %collective-permute-done.1 = bf16[2,64,2560]{2,1,0:T(8,128)(2,1)} collective-permute-done((bf16[2,64,2560]{2,1,0:T(8,128)(2,1)}, bf16[2,64,2560]{2,1,0:T(8,128)(2,1)}, u32[]{:S(2)}, u32[]{:S(2)}) %collective-permute-start.1) | collective-permute-done | bytes 655392 | tf_op jit(solution)/shard_map/ppermute | solution.py:20
  250.9 1.8 fusion.98
  252.7 1.2 concatenate.89
  256.1 3.5 %fusion.102 = (f32[20,64]{1,0:T(8,128)S(1)}, f32[20,64,192]{2,1,0:T(8,128)}) fusion(bf16[64,20,128]{2,0,1:T(8,128)(2,1)} %copy.32, bf16[64,20,128]{2,0,1:T(8,128)(2,1)} %copy.31, bf16[64,20,64]{2,0,1:T(8,128)(2,1)} %get-tuple-element.33, bf16[64,20,64]{2,0,1:T(8,128)(2,1)} %get-tuple-element.34, pred[192]{0:T(512)(128)(4,1)S(1)} %copy-done.16, ...), kind=kOutput, calls=%fused_computation.168 | convolution fusion | flops 68485312 | bytes 2299072 | tf_op jit(solution)/shard_map/sub | solution.py:76
  259.5 1.9 fusion.11
  262.9 7.3 %multiply_reduce_fusion = (f32[64]{0:T(128)S(1)}, f32[64,2560]{1,0:T(8,128)S(1)}) fusion(bf16[2560,2560]{1,0:T(8,128)(2,1)} %all-gather.3.cloned.1.call-done, bf16[64,2560]{1,0:T(8,128)(2,1)S(1)} %get-tuple-element.6, f32[2560]{0:T(1024)S(1)} %get-tuple-element.38, f32[2560]{0:T(1024)S(1)} %get-tuple-element.39, f32[64]{0:T(128)S(1)} %add_rsqrt_fusion.2, ...), kind=kOutput, calls=%fused_computation.71 | convolution fusion | flops 840171456 | bytes 14111488 | tf_op jit(solution)/shard_map/dot_general | solution.py:162
  271.3 1.2 reshape.307
  272.4 1.4 fusion.93
  273.8 7.3 %multiply_reduce_fusion.1 = (f32[64]{0:T(128)S(1)}, f32[64,2560]{1,0:T(8,128)S(1)}) fusion(bf16[2560,2560]{1,0:T(8,128)(2,1)} %all-gather.5.cloned.1.call-done, bf16[64,2560]{1,0:T(8,128)(2,1)S(1)} %get-tuple-element.6, f32[2560]{0:T(1024)S(1)} %get-tuple-element.38, f32[2560]{0:T(1024)S(1)} %get-tuple-element.39, f32[64]{0:T(128)S(1)} %add_rsqrt_fusion.2, ...), kind=kOutput, calls=%fused_computation.75 | convolution fusion | flops 840171456 | bytes 14111488 | tf_op jit(solution)/shard_map/dot_general | solution.py:161
  282.1 1.2 reshape.306
  284.7 1.2 subtract_convert_fusion.1
  285.9 3.2 %fusion.105 = (f32[20,64]{1,0:T(8,128)S(1)}, f32[20,64,192]{2,1,0:T(8,128)}) fusion(bf16[64,20,128]{2,0,1:T(8,128)(2,1)} %copy.32, bf16[64,20,128]{2,0,1:T(8,128)(2,1)} %copy.31, bf16[64,20,64]{2,0,1:T(8,128)(2,1)S(1)} %get-tuple-element.31, bf16[64,20,64]{2,0,1:T(8,128)(2,1)} %get-tuple-element.32, pred[192]{0:T(512)(128)(4,1)S(1)} %copy-done.16, ...), kind=kOutput, calls=%fused_computation.169 | convolution fusion | flops 68485312 | bytes 2299072 | tf_op jit(solution)/shard_map/sub | solution.py:76
  289.1 2.1 fusion.9
  (92 shorter events, 23.6 us)
Async XLA Ops:
  6.5 18.3 %copy-start = (bf16[128,7680]{1,0:T(8,128)(2,1)S(1)}, bf16[128,7680]{1,0:T(8,128)(2,1)}, u32[]{:S(2)}) copy-start(bf16[128,7680]{1,0:T(8,128)(2,1)} %param.17) | copy-start | bytes 5898244
  6.5 18.0 %copy-start.3 = (bf16[64,2560]{1,0:T(8,128)(2,1)S(1)}, bf16[64,2560]{1,0:T(8,128)(2,1)}, u32[]{:S(2)}) copy-start(bf16[64,2560]{1,0:T(8,128)(2,1)} %param.11) | copy-start | bytes 983044
  6.5 102.6 %all-gather.3.cloned.1.call-start = ((), (), s32[]{:S(2)}) async-start(), calls=%async_computation | async-start | bytes 13516800 | tf_op jit(solution)/shard_map/all_gather | solution.py:131
  7.3 201.0 %all-gather.5.cloned.1.call-start = ((), (), s32[]{:S(2)}) async-start(), calls=%async_computation.1 | async-start | bytes 13516800 | tf_op jit(solution)/shard_map/all_gather | solution.py:130
  24.8 84.4 %copy-start.2 = (bf16[64,2560]{1,0:T(8,128)(2,1)S(1)}, bf16[64,2560]{1,0:T(8,128)(2,1)}, u32[]{:S(2)}) copy-start(bf16[64,2560]{1,0:T(8,128)(2,1)} %param.10) | copy-start | bytes 983044
  109.2 8.5 %copy-start.1 = (bf16[2560,2560]{1,0:T(8,128)(2,1)S(1)}, bf16[2560,2560]{1,0:T(8,128)(2,1)}, u32[]{:S(2)}) copy-start(bf16[2560,2560]{1,0:T(8,128)(2,1)} %all-gather.3.cloned.1.call-done) | copy-start | bytes 39321604
  117.6 2.6 copy-start.14
  127.5 88.1 %copy-start.15 = (f32[2560]{0:T(1024)S(1)}, f32[2560]{0:T(1024)}, u32[]{:S(2)}) copy-start(f32[2560]{0:T(1024)} %param.18) | copy-start | bytes 30724
  217.8 1.1 copy-start.4
  217.8 1.4 copy-start.5
  217.8 1.6 copy-start.6
  217.8 1.8 copy-start.7
  221.4 1.0 copy-start.10
  223.3 13.8 %collective-permute-start = (bf16[2,64,2560]{2,1,0:T(8,128)(2,1)}, bf16[2,64,2560]{2,1,0:T(8,128)(2,1)S(1)}, u32[]{:S(2)}, u32[]{:S(2)}) collective-permute-start(bf16[2,64,2560]{2,1,0:T(8,128)(2,1)} %pad_maximum_fusion.12), channel_id=1, source_target_pairs={{0,1},{1,2},{2,3},{3,4},{4,5},{5,6},{6,7},{7,8},{8,9},{9,10},{10,1... | collective-permute-start | bytes 1966088 | tf_op jit(solution)/shard_map/ppermute | solution.py:20
  228.0 22.9 %collective-permute-start.1 = (bf16[2,64,2560]{2,1,0:T(8,128)(2,1)}, bf16[2,64,2560]{2,1,0:T(8,128)(2,1)}, u32[]{:S(2)}, u32[]{:S(2)}) collective-permute-start(bf16[2,64,2560]{2,1,0:T(8,128)(2,1)} %pad_maximum_fusion.12), channel_id=1, source_target_pairs={{0,2},{1,3},{2,4},{3,5},{4,6},{5,7},{6,8},{7,9},{8,10},{9,11},{10,... | collective-permute-start | bytes 1966088 | tf_op jit(solution)/shard_map/ppermute | solution.py:20
  253.9 2.1 copy-start.16
  254.9 1.1 copy-start.11
  256.0 3.5 %copy-start.13 = (bf16[64,20,128]{2,0,1:T(8,128)(2,1)}, bf16[64,20,128]{2,0,1:T(8,128)(2,1)S(1)}, u32[]{:S(2)}) copy-start(bf16[64,20,128]{2,0,1:T(8,128)(2,1)S(1)} %copy.26) | copy-start | bytes 983044
  256.0 3.5 %copy-start.12 = (bf16[64,20,128]{2,0,1:T(8,128)(2,1)S(1)}, bf16[64,20,128]{2,0,1:T(8,128)(2,1)}, u32[]{:S(2)}) copy-start(bf16[64,20,128]{2,0,1:T(8,128)(2,1)} %copy.25) | copy-start | bytes 983044
  283.3 1.1 copy-start.8
  283.3 1.4 copy-start.9
Sparse Core Ops, SparseCore 0:
  10.2 98.9 all-gather.2
  112.0 96.2 all-gather.4
where the time goes:
time: 300 us; the launch traced here: 299 us
  waiting for transfers between devices  183 us (61%)
  matrix products  43.8 us (15%)
  local copies, waits for them, and re-layouts  26.6 us (9%)
  between operations  19.9 us (7%)
  other arithmetic  19.1 us (6%)
  starting transfers between devices  6.54 us (2%)
    all_gather x1, waiting for transfers between devices, local(): lax.all_gather(w_key, 'fsdp', axis=0, tiled=True)  82.3 us
    all_gather x1, waiting for transfers between devices, local(): lax.all_gather(w_query, 'fsdp', axis=0, tiled=True)  80.8 us
    ppermute x2, waiting for transfers between devices, passed_along(): lax.ppermute(value, axis, [(source, source + steps) for source in range(l...  18.6 us
    dot_general x1, matrix products, absorb_both(): jnp.dot(noisy_hidden, pieces[1], preferred_element_type=jnp.float32)  7.43 us
    dot_general x1, matrix products, local(): query_raw = jnp.dot(hidden, full_query, preferred_element_type=jnp.float32)  7.28 us
    dot_general x1, matrix products, absorb_both(): jnp.dot(noisy_hidden, pieces[0], preferred_element_type=jnp.float32)  7.28 us
    dot_general x1, matrix products, local(): key_raw = jnp.dot(hidden, full_key, preferred_element_type=jnp.float32)  7.28 us
    sub x2, matrix products, attend(): expanded = jnp.exp(scores - highest)  6.65 us
  transfers between devices with their start and end apart: 4, of which 4 were waited for; matrix products, arithmetic and copies ran while one was open for 11% of the time, Pallas kernels for 0%

commit v1 on v0

--- a/solution.py
+++ b/solution.py
@@ -127,7 +127,15 @@
     buffers, partials = absorb_both(
         ((empty_buffer, empty_buffer), (empty_sum, empty_sum, empty_sum)),
         (
-            lax.all_gather(w_query, "fsdp", axis=0, tiled=True),
+            jnp.concatenate(
+                lax.all_to_all(
+                    jnp.stack([w_query] * lax.axis_size("fsdp"), axis=0),
+                    concat_axis=0,
+                    axis_name="fsdp",
+                    split_axis=0,
+                ),
+                axis=0,
+            ),
             lax.all_gather(w_key, "fsdp", axis=0, tiled=True),
         ),
         jnp.int32(0),

time: 300 us -> 449 us (1.50)
  waiting for transfers between devices: 183 us -> 328 us
  starting transfers between devices: 6.54 us -> 13.7 us
    all_gather x1, waiting for transfers between devices: 82.3 us -> 199 us  [local(): lax.all_gather(w_key, 'fsdp', axis=0, tiled=True)]
    all_to_all x0 -> x1, waiting for transfers between devices: none -> 112 us  [local(): lax.all_to_all(jnp.stack([w_query] * lax.axis_size('fsdp'), axis=0), conc...]
    all_gather x1 -> x0, waiting for transfers between devices: 80.8 us -> none  [local(): lax.all_gather(w_query, 'fsdp', axis=0, tiled=True)]
    another operation x0 -> x1, local copies, waits for them, and re-layouts: none -> 7.2 us  [local(): jnp.stack([w_query] * lax.axis_size('fsdp'), axis=0)]
    all_to_all x0 -> x1, starting transfers between devices: none -> 6.38 us  [local(): lax.all_to_all(jnp.stack([w_query] * lax.axis_size('fsdp'), axis=0), conc...]
  transfers between devices with their start and end apart: 4 -> 4, of which waited for: 4 -> 4; matrix products, arithmetic and copies ran while one was open for 11% -> 8% of each run, Pallas kernels for 0% -> 0%
where the time goes in v1:
time: 449 us; the launch traced here: 444 us
  waiting for transfers between devices  328 us (73%)
  matrix products  43.5 us (10%)
  local copies, waits for them, and re-layouts  25.1 us (6%)
  between operations  19.4 us (4%)
  other arithmetic  14.7 us (3%)
  starting transfers between devices  13.7 us (3%)
    all_gather x1, waiting for transfers between devices, local(): lax.all_gather(w_key, 'fsdp', axis=0, tiled=True)  199 us
    all_to_all x1, waiting for transfers between devices, local(): lax.all_to_all(jnp.stack([w_query] * lax.axis_size('fsdp'), axis=0), conc...  112 us
    ppermute x2, waiting for transfers between devices, passed_along(): lax.ppermute(value, axis, [(source, source + steps) for source in range(l...  15.2 us
  transfers between devices with their start and end apart: 4, of which 4 were waited for; matrix products, arithmetic and copies ran while one was open for 8% of the time, Pallas kernels for 0%

profile of v1, /device:TPU:9, one launch (start us, length us, event | category | flops | bytes accessed | tf_op | source)
XLA Modules:
  0.0 444.1 jit_solution(16683767625793898510)
XLA Ops:
  7.3 7.2 %stack.8 = bf16[32,80,2560]{2,1,0:T(8,128)(2,1)} broadcast(bf16[80,2560]{1,0:T(8,128)(2,1)} %param.15), dimensions={1,2} | broadcast | bytes 13516800 | tf_op jit(solution)/shard_map/stack | solution.py:132
  14.5 6.4 %all-to-all-start = ((bf16[32,80,2560]{2,1,0:T(8,128)(2,1)}), bf16[32,80,2560]{2,1,0:T(8,128)(2,1)}, u32[]{:S(2)}, u32[]{:S(2)}) async-start(bf16[32,80,2560]{2,1,0:T(8,128)(2,1)} %stack.8), calls=%async_computation | async-start | bytes 26214400 | tf_op jit(solution)/shard_map/all_to_all | solution.py:131
  23.5 1.2 fusion.50
  33.6 199.3 %all-gather.2.cloned.1.call-done = bf16[2560,2560]{1,0:T(8,128)(2,1)} async-done(((bf16[80,2560]{1,0:T(8,128)(2,1)}), bf16[2560,2560]{1,0:T(8,128)(2,1)}) %all-gather.2.cloned.1.call-update) | async-done | bytes 13107216 | tf_op jit(solution)/shard_map/all_gather | solution.py:139
  233.0 7.4 %multiply_reduce_fusion.2 = (f32[64]{0:T(128)S(1)}, f32[64,2560]{1,0:T(8,128)S(1)}) fusion(bf16[2560,2560]{1,0:T(8,128)(2,1)} %all-gather.2.cloned.1.call-done, bf16[64,2560]{1,0:T(8,128)(2,1)S(1)} %copy-done.3, f32[2560]{0:T(1024)S(1)} %get-tuple-element.41, f32[2560]{0:T(1024)S(1)} %get-tuple-element.42, f32[64]{0:T(128)S(1)} %add_rsqrt_fusion.7, ...), kind=kOutput, calls=%fused_computation.79 | convolution fusion | flops 840171456 | bytes 14111488 | tf_op jit(solution)/shard_map/dot_general | solution.py:87
  240.4 1.0 copy-done.2
  241.4 2.5 multiply_reduce_fusion.4
  244.0 0.9 multiply_multiply_fusion.2
  244.9 1.0 reshape.311
  245.9 1.2 reshape.308
  247.1 2.8 fusion.95
  249.8 1.4 fusion.96
  251.3 112.5 %all-to-all-done = bf16[32,80,2560]{2,1,0:T(8,128)(2,1)} async-done(((bf16[32,80,2560]{2,1,0:T(8,128)(2,1)}), bf16[32,80,2560]{2,1,0:T(8,128)(2,1)}, u32[]{:S(2)}, u32[]{:S(2)}) %all-to-all-start) | async-done | bytes 13107232 | tf_op jit(solution)/shard_map/all_to_all | solution.py:131
  363.8 7.3 %multiply_reduce_fusion.3 = (f32[64]{0:T(128)S(1)}, f32[64,2560]{1,0:T(8,128)S(1)}) fusion(bf16[2560,2560]{1,0:T(8,128)(2,1)} %bitcast.10, bf16[64,2560]{1,0:T(8,128)(2,1)S(1)} %copy-done.3, f32[2560]{0:T(1024)S(1)} %get-tuple-element.41, f32[2560]{0:T(1024)S(1)} %get-tuple-element.42, f32[64]{0:T(128)S(1)} %add_rsqrt_fusion.7, ...), kind=kOutput, calls=%fused_computation.83 | convolution fusion | flops 840171456 | bytes 14111488 | tf_op jit(solution)/shard_map/dot_general | solution.py:86
  371.1 1.0 multiply_multiply_fusion.3
  372.1 1.2 reshape.310
  375.1 1.8 subtract_convert_fusion.3
  377.5 0.9 pad_maximum_fusion.12
  378.4 3.0 collective-permute-start.1
  382.5 1.0 copy_bitcast_fusion.1
  383.5 4.3 collective-permute-start
  387.8 12.2 %collective-permute-done.1 = bf16[2,64,2560]{2,1,0:T(8,128)(2,1)S(1)} collective-permute-done((bf16[2,64,2560]{2,1,0:T(8,128)(2,1)}, bf16[2,64,2560]{2,1,0:T(8,128)(2,1)S(1)}, u32[]{:S(2)}, u32[]{:S(2)}) %collective-permute-start.1) | collective-permute-done | bytes 655392 | tf_op jit(solution)/shard_map/ppermute | solution.py:20
  400.3 3.0 collective-permute-done
  406.5 3.1 fusion.102
  409.6 1.9 fusion.11
  412.0 1.0 copy_bitcast_fusion
  413.0 7.3 %multiply_reduce_fusion.1 = (f32[64]{0:T(128)S(1)}, f32[64,2560]{1,0:T(8,128)S(1)}) fusion(bf16[2560,2560]{1,0:T(8,128)(2,1)} %bitcast.10, bf16[64,2560]{1,0:T(8,128)(2,1)S(1)} %get-tuple-element.6, f32[2560]{0:T(1024)S(1)} %get-tuple-element.38, f32[2560]{0:T(1024)S(1)} %get-tuple-element.39, f32[64]{0:T(128)S(1)} %add_rsqrt_fusion.2, ...), kind=kOutput, calls=%fused_computation.75 | convolution fusion | flops 840171456 | bytes 14111488 | tf_op jit(solution)/shard_map/dot_general | solution.py:169
  420.8 7.3 %multiply_reduce_fusion = (f32[64]{0:T(128)S(1)}, f32[64,2560]{1,0:T(8,128)S(1)}) fusion(bf16[2560,2560]{1,0:T(8,128)(2,1)} %all-gather.2.cloned.1.call-done, bf16[64,2560]{1,0:T(8,128)(2,1)S(1)} %get-tuple-element.6, f32[2560]{0:T(1024)S(1)} %get-tuple-element.38, f32[2560]{0:T(1024)S(1)} %get-tuple-element.39, f32[64]{0:T(128)S(1)} %add_rsqrt_fusion.2, ...), kind=kOutput, calls=%fused_computation.71 | convolution fusion | flops 840171456 | bytes 14111488 | tf_op jit(solution)/shard_map/dot_general | solution.py:170
  428.1 1.0 multiply_multiply_fusion
  429.1 1.2 reshape.313
  431.1 3.1 fusion.105
  434.2 2.2 fusion.9
  (108 shorter events, 16.2 us)
Async XLA Ops:
  6.5 25.2 %copy-start = (bf16[128,7680]{1,0:T(8,128)(2,1)S(1)}, bf16[128,7680]{1,0:T(8,128)(2,1)}, u32[]{:S(2)}) copy-start(bf16[128,7680]{1,0:T(8,128)(2,1)} %param.17) | copy-start | bytes 5898244
  6.5 226.4 %all-gather.2.cloned.1.call-start = ((), (), s32[]{:S(2)}) async-start(), calls=%async_computation.1 | async-start | bytes 13516800 | tf_op jit(solution)/shard_map/all_gather | solution.py:139
  14.5 6.4 %copy-start.20 = (s32[1,2]{1,0:T(1,128)S(1)}, s32[1,2]{1,0:T(1,128)}, u32[]{:S(2)}) copy-start(s32[1,2]{1,0:T(1,128)} %param.14) | copy-start | bytes 28
  14.5 8.4 %copy-start.19 = (s32[32]{0:T(128)S(1)}, s32[32]{0:T(128)}, u32[]{:S(2)}) copy-start(s32[32]{0:T(128)} %param.12) | copy-start | bytes 388
  14.5 13.2 %copy-start.21 = (s32[1,2]{1,0:T(1,128)S(1)}, s32[1,2]{1,0:T(1,128)}, u32[]{:S(2)}) copy-start(s32[1,2]{1,0:T(1,128)} %param.13) | copy-start | bytes 28
  14.5 16.4 %copy-start.4 = (bf16[64,2560]{1,0:T(8,128)(2,1)S(1)}, bf16[64,2560]{1,0:T(8,128)(2,1)}, u32[]{:S(2)}) copy-start(bf16[64,2560]{1,0:T(8,128)(2,1)} %param.11) | copy-start | bytes 983044
  14.5 16.5 %copy-start.3 = (bf16[64,2560]{1,0:T(8,128)(2,1)S(1)}, bf16[64,2560]{1,0:T(8,128)(2,1)}, u32[]{:S(2)}) copy-start(bf16[64,2560]{1,0:T(8,128)(2,1)} %param.10) | copy-start | bytes 983044
  14.5 349.3 %all-to-all-start = ((bf16[32,80,2560]{2,1,0:T(8,128)(2,1)}), bf16[32,80,2560]{2,1,0:T(8,128)(2,1)}, u32[]{:S(2)}, u32[]{:S(2)}) async-start(bf16[32,80,2560]{2,1,0:T(8,128)(2,1)} %stack.8), calls=%async_computation | async-start | bytes 26214400 | tf_op jit(solution)/shard_map/all_to_all | solution.py:131
  233.0 8.5 %copy-start.2 = (bf16[2560,2560]{1,0:T(8,128)(2,1)S(1)}, bf16[2560,2560]{1,0:T(8,128)(2,1)}, u32[]{:S(2)}) copy-start(bf16[2560,2560]{1,0:T(8,128)(2,1)} %all-gather.2.cloned.1.call-done) | copy-start | bytes 39321604
  241.4 2.6 copy-start.16
  363.8 7.3 %copy-start.15 = (f32[2560]{0:T(1024)S(1)}, f32[2560]{0:T(1024)}, u32[]{:S(2)}) copy-start(f32[2560]{0:T(1024)} %param.18) | copy-start | bytes 30724
  373.3 1.1 copy-start.5
  373.3 1.4 copy-start.6
  373.3 1.6 copy-start.7
  373.3 1.8 copy-start.8
  376.9 4.6 %copy-start.22 = (bf16[64]{0:T(256)(128)(2,1)S(1)}, bf16[64]{0:T(256)(128)(2,1)}, u32[]{:S(2)}) copy-start(bf16[64]{0:T(256)(128)(2,1)} %get-tuple-element.74) | copy-start | bytes 388
  376.9 4.6 %copy-start.23 = (bf16[64]{0:T(256)(128)(2,1)S(1)}, bf16[64]{0:T(256)(128)(2,1)}, u32[]{:S(2)}) copy-start(bf16[64]{0:T(256)(128)(2,1)} %get-tuple-element.75) | copy-start | bytes 388
  378.4 21.6 %collective-permute-start.1 = (bf16[2,64,2560]{2,1,0:T(8,128)(2,1)}, bf16[2,64,2560]{2,1,0:T(8,128)(2,1)S(1)}, u32[]{:S(2)}, u32[]{:S(2)}) collective-permute-start(bf16[2,64,2560]{2,1,0:T(8,128)(2,1)} %pad_maximum_fusion.12), channel_id=1, source_target_pairs={{0,2},{1,3},{2,4},{3,5},{4,6},{5,7},{6,8},{7,9},{8,10},{9,11},{10,... | collective-permute-start | bytes 1966088 | tf_op jit(solution)/shard_map/ppermute | solution.py:20
  383.5 19.8 %collective-permute-start = (bf16[2,64,2560]{2,1,0:T(8,128)(2,1)}, bf16[2,64,2560]{2,1,0:T(8,128)(2,1)S(1)}, u32[]{:S(2)}, u32[]{:S(2)}) collective-permute-start(bf16[2,64,2560]{2,1,0:T(8,128)(2,1)} %pad_maximum_fusion.12), channel_id=1, source_target_pairs={{0,1},{1,2},{2,3},{3,4},{4,5},{5,6},{6,7},{7,8},{8,9},{9,10},{10,1... | collective-permute-start | bytes 1966088 | tf_op jit(solution)/shard_map/ppermute | solution.py:20
  400.3 9.3 %copy-start.13 = (bf16[64,20,128]{2,0,1:T(8,128)(2,1)}, bf16[64,20,128]{2,0,1:T(8,128)(2,1)S(1)}, u32[]{:S(2)}) copy-start(bf16[64,20,128]{2,0,1:T(8,128)(2,1)S(1)} %copy.26) | copy-start | bytes 983044
  403.6 2.9 copy-start.9
  403.6 2.9 copy-start.10
  403.6 2.9 copy-start.11
  403.6 2.9 copy-start.12
  403.6 2.8 copy-start.24
  406.5 3.1 copy-start.14
  409.6 1.9 copy-start.17
  434.2 2.2 copy-start.18
  434.2 3.1 copy-start.1
Sparse Core Ops, SparseCore 0:
  10.2 222.7 all-gather.1
